TPU v7x, 256 devices: a whole 4x4x8 slice. The times are simulated.
256 devices in a mesh: rep: 16 (over z_lo, x), tp: 16 (over y, z_hi, core).
Axes of the slice: x: 4, y: 4, z: 8 (z_hi: 2, z_lo: 4; z = z_hi * 4 + z_lo), core: 2. Of those that a mesh axis runs over, the one named last changes fastest.
Arguments:
- queries: bfloat16 [16, 512, 4096], P('rep', None, 'tp'), may hold values from -120 to 120
- keys: bfloat16 [16, 512, 4096], P('rep', None, 'tp'), may hold values from -6 to 6
- values: bfloat16 [16, 512, 4096], P('rep', None, 'tp'), may hold values from -6 to 6
- out_weight: bfloat16 [16, 4096, 7168], P('rep', 'tp'), may hold values from -0.09375 to 0.09375
- cotangent: bfloat16 [16, 512, 7168], P('rep', 'tp'), may hold values from -6 to 6
- local_params: bfloat16 [16, 2, 128, 7168], P('rep', None, 'tp'), may hold values from -6 to 6
- global_params: float32 [2, 128, 7168], P(None, 'tp'), may hold values from -6 to 6
- momentum: float32 [2, 128, 7168], P(None, 'tp'), may hold values from -3 to 3
- frag_index: int32 [1], replicated, may hold values from 0 to 1
Outputs:
- branch_out: bfloat16 [16, 512, 7168], P('rep', 'tp')
- weight_grad: bfloat16 [16, 4096, 7168], P('rep', 'tp')
- query_grad: bfloat16 [16, 512, 4096], P('rep', None, 'tp')
- key_grad: bfloat16 [16, 512, 4096], P('rep', None, 'tp')
- value_grad: bfloat16 [16, 512, 4096], P('rep', None, 'tp')
- new_global: float32 [128, 7168], P('tp')
- new_momentum: float32 [128, 7168], P('tp')
All inputs are finite; a program needn't handle non-finite values.
Results may differ from a plain program's by a relative error of at most 0.017.
Values may be sent and summed in bfloat16 or wider, within the bound.
No kernel may reach another device: no remote copies, remote signals or barrier semaphores. Data moves between devices by JAX's collectives and lax.ppermute only.
A program may use at most 128 MiB of HBM per device.

v0:
```python
import jax
import jax.numpy as jnp
from jax import lax
from jax.sharding import PartitionSpec as P

HD = 128
LEN = 512
SEQS = 1
outer_momentum = 0.9
outer_rate = 0.7


def nesterov(outer_old, moment_old, summed):
    average = summed / lax.axis_size("rep")
    pseudo_grad = outer_old - average
    new_momentum = outer_momentum * moment_old + pseudo_grad
    new_global = outer_old - outer_rate * (outer_momentum * new_momentum + pseudo_grad)
    return (new_global, new_momentum)


def outer_update(local_params, global_params, momentum, frag_index):
    chosen = frag_index[0]
    local_sel = lax.dynamic_index_in_dim(local_params[0], chosen, 0, keepdims=False).astype(
        jnp.float32
    )
    outer_old = lax.dynamic_index_in_dim(global_params, chosen, 0, keepdims=False)
    moment_old = lax.dynamic_index_in_dim(momentum, chosen, 0, keepdims=False)
    summed = lax.psum(local_sel.astype(jnp.bfloat16), "rep").astype(jnp.float32)
    return nesterov(outer_old, moment_old, summed)


def inner_step(queries, keys, values, out_weight, cotangent):
    scale = HD ** (-0.5)
    head_cols = queries.shape[2]
    heads_here = head_cols // HD
    tokens = queries.shape[1]
    weight_here = out_weight[0]
    query_heads = queries[0].reshape(SEQS, LEN, heads_here, HD)
    key_heads = keys[0].reshape(SEQS, LEN, heads_here, HD)
    value_heads = values[0].reshape(SEQS, LEN, heads_here, HD)
    scores = (
        jnp.einsum("slhd,smhd->shlm", query_heads, key_heads, preferred_element_type=jnp.float32)
        * scale
    )
    causal = jnp.arange(LEN)[:, None] >= jnp.arange(LEN)[None, :]
    scores = jnp.where(causal[None, None], scores, -1e30)
    top = jnp.max(scores, axis=-1, keepdims=True)
    weights = jnp.exp(scores - top)
    probs = weights / jnp.sum(weights, axis=-1, keepdims=True)
    probs_half = probs.astype(jnp.bfloat16)
    context = jnp.einsum(
        "shlm,smhd->slhd", probs_half, value_heads, preferred_element_type=jnp.float32
    )
    context = context.astype(jnp.bfloat16).reshape(tokens, head_cols)
    context_rows = context
    branch_out = lax.psum_scatter(
        jnp.dot(context_rows, weight_here, preferred_element_type=jnp.float32).astype(jnp.bfloat16),
        "tp",
        scatter_dimension=0,
        tiled=True,
    )
    block_rows = lax.all_gather(cotangent[0], "tp", axis=0, tiled=True)
    part_grad = lax.dot_general(
        block_rows, weight_here, (((1,), (1,)), ((), ())), preferred_element_type=jnp.float32
    )
    context_acc = part_grad
    context_rows = context
    weight_acc = lax.dot_general(
        context_rows, block_rows, (((0,), (0,)), ((), ())), preferred_element_type=jnp.float32
    )
    context_acc, weight_acc = (context_acc, weight_acc)
    weight_grad = weight_acc.astype(jnp.bfloat16)
    context_grad = context_acc.astype(jnp.bfloat16).reshape(SEQS, LEN, heads_here, HD)
    probs_grad = jnp.einsum(
        "slhd,smhd->shlm", context_grad, value_heads, preferred_element_type=jnp.float32
    )
    inner = jnp.sum(probs * probs_grad, axis=-1, keepdims=True)
    score_grad = (probs * (probs_grad - inner) * scale).astype(jnp.bfloat16)
    query_grad = jnp.einsum(
        "shlm,smhd->slhd", score_grad, key_heads, preferred_element_type=jnp.float32
    )
    key_grad = jnp.einsum(
        "shlm,slhd->smhd", score_grad, query_heads, preferred_element_type=jnp.float32
    )
    value_grad = jnp.einsum(
        "shlm,slhd->smhd", probs_half, context_grad, preferred_element_type=jnp.float32
    )
    shaped = [
        g.astype(jnp.bfloat16).reshape(1, tokens, head_cols)
        for g in (query_grad, key_grad, value_grad)
    ]
    return (branch_out[None], weight_grad[None], shaped[0], shaped[1], shaped[2])


def shards(
    queries, keys, values, out_weight, cotangent, local_params, global_params, momentum, frag_index
):
    results = inner_step(queries, keys, values, out_weight, cotangent)
    new_global, new_momentum = outer_update(local_params, global_params, momentum, frag_index)
    return (results[0], results[1], results[2], results[3], results[4], new_global, new_momentum)


def solution(mesh):
    placed = (
        P("rep", None, "tp"),
        P("rep", None, "tp"),
        P("rep", None, "tp"),
        P("rep", "tp", None),
        P("rep", "tp", None),
        P("rep", None, "tp", None),
        P(None, "tp", None),
        P(None, "tp", None),
        P(),
    )
    return jax.shard_map(
        shards,
        mesh=mesh,
        in_specs=placed,
        out_specs=(
            P("rep", "tp", None),
            P("rep", "tp", None),
            P("rep", None, "tp"),
            P("rep", None, "tp"),
            P("rep", None, "tp"),
            P("tp", None),
            P("tp", None),
        ),
        check_vma=False,
    )
```

profile of v0, /device:TPU:128, one launch (start us, length us, event | category | flops | bytes accessed | tf_op | source)
XLA Modules:
  0.0 294.4 jit_solution(1788196400667213289)
XLA Ops:
  8.0 0.0 copy-start
  8.0 0.0 all-reduce.2.cloned.1.call-start
  8.8 0.2 copy-done
  8.9 0.7 dynamic-slice_bitcast_fusion
  9.6 0.0 all-reduce.2.cloned.1.call-update
  9.6 0.0 all-gather.3.cloned.1.call-start
  9.7 0.5 all-gather.3.cloned.1.call-update
  10.2 0.0 reduce-scatter.2.cloned.1.call-start
  10.2 1.1 copy.35
  11.3 1.1 copy.36
  12.4 0.0 copy-start.1
  12.5 1.1 reshape.115
  13.6 0.1 iota_compare_fusion
  13.7 0.0 copy-start.2
  13.7 2.3 fusion.47
  16.0 0.0 copy-done.1
  16.0 0.0 copy-done.2
  16.0 1.3 convolution_convert_fusion.2
  17.3 7.2 %convolution_convert_fusion = bf16[512,7168]{1,0:T(8,128)(2,1)} fusion(bf16[512,256]{0,1:T(8,128)(2,1)S(1)} %bitcast.75, bf16[1,256,7168]{2,1,0:T(8,128)(2,1)} %param.12), kind=kOutput, calls=%fused_computation.2 | convolution fusion | flops 1882718208 | bytes 11272192 | tf_op jit(solution)/shard_map/dot_general | solution.py:57
  24.5 0.0 reduce-scatter.2.cloned.1.call-update
  24.5 235.7 %all-reduce.2.cloned.1.call-done = bf16[8,7168]{1,0:T(8,128)(2,1)} async-done(((bf16[8,7168]{1,0:T(8,128)(2,1)}), bf16[8,7168]{1,0:T(8,128)(2,1)}) %all-reduce.2.cloned.1.call-update) | async-done | bytes 114704 | tf_op jit(solution)/shard_map/psum | solution.py:28
  260.2 0.0 copy-done.4
  260.2 1.7 bitcast_subtract_fusion
  262.0 6.2 %fusion.24 = bf16[512,256]{0,1:T(8,128)(2,1)S(1)} fusion(bf16[1,256,7168]{2,1,0:T(8,128)(2,1)} %param.12, bf16[1,512,7168]{2,1,0:T(8,128)(2,1)} %all-gather.3.cloned.1.call-done), kind=kOutput, calls=%fused_computation.20 | convolution fusion | flops 1879179264 | bytes 11272192 | tf_op jit(solution)/shard_map/dot_general | solution.py:63
  268.2 0.4 fusion.37
  268.6 3.3 %fusion.18 = bf16[2,512,128]{1,2,0:T(8,128)(2,1)S(1)} fusion(bf16[512,2,128]{0,2,1:T(8,128)(2,1)} %bitcast.85, f32[2,512,512]{1,2,0:T(8,128)S(1)} %fusion.37, f32[2,512,512]{1,2,0:T(8,128)} %get-tuple-element.17, f32[2,512]{1,0:T(2,128)S(1)} %get-tuple-element.16), kind=kOutput, calls=%fused_computation.18 | convolution fusion | flops 138020352 | bytes 4722688 | tf_op jit(solution)/shard_map/shlm,smhd->slhd/dot_general | solution.py:79
  271.9 0.8 copy.27
  272.8 3.1 %fusion.21 = bf16[2,512,128]{1,2,0:T(8,128)(2,1)S(1)} fusion(bf16[512,2,128]{0,2,1:T(8,128)(2,1)S(1)} %bitcast.81, f32[2,512,512]{1,2,0:T(8,128)S(1)} %fusion.37, f32[2,512,512]{1,2,0:T(8,128)} %get-tuple-element.17, f32[2,512]{1,0:T(2,128)S(1)} %get-tuple-element.16), kind=kOutput, calls=%fused_computation.19 | convolution fusion | flops 138020352 | bytes 4722688 | tf_op jit(solution)/shard_map/shlm,slhd->smhd/dot_general | solution.py:82
  275.9 0.8 copy.28
  276.7 2.4 convolution_convert_fusion.3
  279.1 0.8 copy.29
  279.9 7.0 %fusion.2 = bf16[1,256,7168]{2,1,0:T(8,128)(2,1)} fusion(bf16[512,256]{0,1:T(8,128)(2,1)S(1)} %bitcast.76, bf16[1,512,7168]{2,1,0:T(8,128)(2,1)} %all-gather.3.cloned.1.call-done), kind=kOutput, calls=%fused_computation.4 | convolution fusion | flops 1880883200 | bytes 11272192 | tf_op jit(solution)/shard_map/dot_general | solution.py:68
  (5 shorter events, 0.0 us)
Async XLA Ops:
  8.0 0.9 copy-start
  8.0 252.2 %all-reduce.2.cloned.1.call-start = ((), (), s32[]{:S(2)}) async-start(), calls=%async_computation.2 | async-start | bytes 229376 | tf_op jit(solution)/shard_map/psum | solution.py:28
  9.6 252.3 %all-gather.3.cloned.1.call-start = ((), (), s32[]{:S(2)}) async-start(), calls=%async_computation.3 | async-start | bytes 7798784 | tf_op jit(solution)/shard_map/all_gather | solution.py:62
  10.2 276.7 %reduce-scatter.2.cloned.1.call-start = ((), (), s32[]{:S(2)}) async-start(), calls=%async_computation.1 | async-start | bytes 7798784 | tf_op jit(solution)/shard_map/reduce_scatter | solution.py:56
  12.4 3.5 %copy-start.1 = (bf16[1,512,256]{1,2,0:T(8,128)(2,1)}, bf16[1,512,256]{1,2,0:T(8,128)(2,1)S(1)}, u32[]{:S(2)}) copy-start(bf16[1,512,256]{1,2,0:T(8,128)(2,1)S(1)} %copy.36) | copy-start | bytes 786436
  13.7 2.3 copy-start.2
  24.5 235.8 %copy-start.3 = (f32[2,8,7168]{2,1,0:T(8,128)S(1)}, f32[2,8,7168]{2,1,0:T(8,128)}, u32[]{:S(2)}) copy-start(f32[2,8,7168]{2,1,0:T(8,128)} %param.15) | copy-start | bytes 1376260
  24.5 235.8 %copy-start.4 = (f32[2,8,7168]{2,1,0:T(8,128)S(1)}, f32[2,8,7168]{2,1,0:T(8,128)}, u32[]{:S(2)}) copy-start(f32[2,8,7168]{2,1,0:T(8,128)} %param.16) | copy-start | bytes 1376260
Sparse Core Ops, SparseCore 0:
  12.2 247.9 all-reduce.1
Sparse Core Ops, SparseCore 1:
  12.8 86.0 all-gather.2
  103.8 130.9 reduce-scatter.1
where the time goes:
time: 295 us; the launch traced here: 294 us
  waiting for transfers between devices  236 us (80%)
  matrix products  33.2 us (11%)
  between operations  16.3 us (6%)
  local copies, waits for them, and re-layouts  6.67 us (2%)
    psum x1, waiting for transfers between devices, outer_update(): summed = lax.psum(local_sel.astype(jnp.bfloat16), 'rep').astype(jnp.float32)  236 us
    dot_general x1, matrix products, inner_step(): jnp.dot(context_rows, weight_here, preferred_element_type=jnp.float32)  7.17 us
    dot_general x1, matrix products, inner_step(): lax.dot_general(context_rows, block_rows, (((0,), (0,)), ((), ())), prefe...  7 us
    dot_general x1, matrix products, inner_step(): lax.dot_general(block_rows, weight_here, (((1,), (1,)), ((), ())), prefer...  6.22 us
  transfers between devices with their start and end apart: 3, of which 1 were waited for; matrix products, arithmetic and copies ran while one was open for 14% of the time, Pallas kernels for 0%

commit v1 on v0

--- a/solution.py
+++ b/solution.py
@@ -25,7 +25,9 @@
     )
     outer_old = lax.dynamic_index_in_dim(global_params, chosen, 0, keepdims=False)
     moment_old = lax.dynamic_index_in_dim(momentum, chosen, 0, keepdims=False)
-    summed = lax.psum(local_sel.astype(jnp.bfloat16), "rep").astype(jnp.float32)
+    summed = jnp.sum(lax.all_gather(local_sel.astype(jnp.bfloat16), "rep"), axis=0).astype(
+        jnp.float32
+    )
     return nesterov(outer_old, moment_old, summed)
 
 

time: 295 us -> 333 us (1.13)
  the two profiles are of different devices: /device:TPU:128 before, /device:TPU:2 now
where the time goes in v1:
time: 333 us
  waiting for transfers between devices  275 us (83%)
  matrix products  34.2 us (10%)
  between operations  14.6 us (4%)
  local copies, waits for them, and re-layouts  6.68 us (2%)
    reduce_scatter x1, waiting for transfers between devices, inner_step(): lax.psum_scatter(jnp.dot(context_rows, weight_here, preferred_element_typ...  103 us
    all_gather x1, waiting for transfers between devices, inner_step(): block_rows = lax.all_gather(cotangent[0], 'tp', axis=0, tiled=True)  99.2 us
    all_gather x1, waiting for transfers between devices, outer_update(): lax.all_gather(local_sel.astype(jnp.bfloat16), 'rep')  72.1 us
    dot_general x1, matrix products, inner_step(): lax.dot_general(context_rows, block_rows, (((0,), (0,)), ((), ())), prefe...  7.61 us
    dot_general x1, matrix products, inner_step(): jnp.dot(context_rows, weight_here, preferred_element_type=jnp.float32)  7.17 us
  transfers between devices with their start and end apart: 3, of which 3 were waited for; matrix products, arithmetic and copies ran while one was open for 13% of the time, Pallas kernels for 0%

profile of v1, /device:TPU:2, one launch (start us, length us, event | category | flops | bytes accessed | tf_op | source)
XLA Modules:
  0.0 333.0 jit_solution(16740651389502273049)
XLA Ops:
  7.2 0.0 copy-start
  7.2 0.0 all-gather.7.cloned.1.call-start
  7.9 0.2 copy-done
  8.1 0.7 constant_dynamic-slice_fusion
  8.8 0.0 all-gather.7.cloned.1.call-update
  8.8 0.0 all-gather.5.cloned.1.call-start
  8.8 0.7 all-gather.5.cloned.1.call-update
  9.5 0.0 reduce-scatter.2.cloned.1.call-start
  9.6 1.1 copy.49
  10.7 1.1 copy.50
  11.8 0.0 copy-start.1
  11.8 1.1 reshape.116
  12.9 0.1 iota_compare_fusion
  13.0 2.3 fusion.47
  15.3 1.3 convolution_convert_fusion.2
  16.6 7.2 %convolution_convert_fusion = bf16[512,7168]{1,0:T(8,128)(2,1)} fusion(bf16[512,256]{0,1:T(8,128)(2,1)S(1)} %bitcast.73, bf16[1,256,7168]{2,1,0:T(8,128)(2,1)} %param.12), kind=kOutput, calls=%fused_computation.2 | convolution fusion | flops 1882718208 | bytes 11272192 | tf_op jit(solution)/shard_map/dot_general | solution.py:59
  23.8 0.0 reduce-scatter.2.cloned.1.call-update
  23.8 0.0 copy-start.4
  23.9 72.1 %all-gather.7.cloned.1.call-done = bf16[16,1,8,7168]{3,2,1,0:T(8,128)(2,1)} async-done(((bf16[1,1,8,7168]{3,2,1,0:T(8,128)(2,1)}), bf16[16,1,8,7168]{3,2,1,0:T(8,128)(2,1)}) %all-gather.7.cloned.1.call-update) | async-done | bytes 1835024 | tf_op jit(solution)/shard_map/all_gather | solution.py:28
  96.0 1.8 reduce_sum.32
  97.8 0.8 bitcast_subtract_fusion
  98.6 99.2 %all-gather.5.cloned.1.call-done = bf16[1,512,7168]{2,1,0:T(8,128)(2,1)} async-done(((bf16[1,32,7168]{2,1,0:T(8,128)(2,1)}), bf16[1,512,7168]{2,1,0:T(8,128)(2,1)}) %all-gather.5.cloned.1.call-update) | async-done | bytes 7340048 | tf_op jit(solution)/shard_map/all_gather | solution.py:64
  197.9 6.2 %fusion.24 = bf16[512,256]{0,1:T(8,128)(2,1)S(1)} fusion(bf16[1,256,7168]{2,1,0:T(8,128)(2,1)} %param.12, bf16[1,512,7168]{2,1,0:T(8,128)(2,1)} %all-gather.5.cloned.1.call-done), kind=kOutput, calls=%fused_computation.20 | convolution fusion | flops 1879179264 | bytes 11272192 | tf_op jit(solution)/shard_map/dot_general | solution.py:65
  204.1 0.4 fusion.37
  204.5 3.3 fusion.18
  207.8 0.8 copy.41
  208.7 3.4 %fusion.21 = bf16[2,512,128]{1,2,0:T(8,128)(2,1)S(1)} fusion(bf16[512,2,128]{0,2,1:T(8,128)(2,1)S(1)} %bitcast.79, f32[2,512,512]{1,2,0:T(8,128)S(1)} %fusion.37, f32[2,512,512]{1,2,0:T(8,128)} %get-tuple-element.24, f32[2,512]{1,0:T(2,128)S(1)} %get-tuple-element.23), kind=kOutput, calls=%fused_computation.19 | convolution fusion | flops 138020352 | bytes 4722688 | tf_op jit(solution)/shard_map/shlm,slhd->smhd/dot_general | solution.py:84
  212.1 0.8 copy.42
  212.9 2.4 convolution_convert_fusion.3
  215.3 0.8 copy.43
  216.2 7.6 %fusion.2 = bf16[1,256,7168]{2,1,0:T(8,128)(2,1)} fusion(bf16[512,256]{0,1:T(8,128)(2,1)S(1)} %bitcast.74, bf16[1,512,7168]{2,1,0:T(8,128)(2,1)} %all-gather.5.cloned.1.call-done), kind=kOutput, calls=%fused_computation.4 | convolution fusion | flops 1880883200 | bytes 11272192 | tf_op jit(solution)/shard_map/dot_general | solution.py:70
  223.8 102.6 %reduce-scatter.2.cloned.1.call-done = bf16[32,7168]{1,0:T(8,128)(2,1)} async-done(((bf16[512,7168]{1,0:T(8,128)(2,1)}), bf16[32,7168]{1,0:T(8,128)(2,1)}) %reduce-scatter.2.cloned.1.call-update) | async-done | bytes 458768 | tf_op jit(solution)/shard_map/reduce_scatter | solution.py:58
  (6 shorter events, 0.0 us)
Async XLA Ops:
  7.2 0.9 copy-start
  7.2 88.8 %all-gather.7.cloned.1.call-start = ((), (), s32[]{:S(2)}) async-start(), calls=%async_computation.3 | async-start | bytes 1949696 | tf_op jit(solution)/shard_map/all_gather | solution.py:28
  8.8 189.1 %all-gather.5.cloned.1.call-start = ((), (), s32[]{:S(2)}) async-start(), calls=%async_computation.2 | async-start | bytes 7798784 | tf_op jit(solution)/shard_map/all_gather | solution.py:64
  9.5 316.9 %reduce-scatter.2.cloned.1.call-start = ((), (), s32[]{:S(2)}) async-start(), calls=%async_computation.1 | async-start | bytes 7798784 | tf_op jit(solution)/shard_map/reduce_scatter | solution.py:58
  11.8 3.5 %copy-start.1 = (bf16[1,512,256]{1,2,0:T(8,128)(2,1)}, bf16[1,512,256]{1,2,0:T(8,128)(2,1)S(1)}, u32[]{:S(2)}) copy-start(bf16[1,512,256]{1,2,0:T(8,128)(2,1)S(1)} %copy.50) | copy-start | bytes 786436
  13.0 2.3 copy-start.2
  23.8 73.9 %copy-start.3 = (f32[2,8,7168]{2,1,0:T(8,128)S(1)}, f32[2,8,7168]{2,1,0:T(8,128)}, u32[]{:S(2)}) copy-start(f32[2,8,7168]{2,1,0:T(8,128)} %param.15) | copy-start | bytes 1376260
  23.8 73.9 %copy-start.4 = (f32[2,8,7168]{2,1,0:T(8,128)S(1)}, f32[2,8,7168]{2,1,0:T(8,128)}, u32[]{:S(2)}) copy-start(f32[2,8,7168]{2,1,0:T(8,128)} %param.16) | copy-start | bytes 1376260
Sparse Core Ops, SparseCore 0:
  10.4 85.5 all-gather.6
  98.7 99.1 all-gather.4
  202.9 123.4 reduce-scatter.1
